TPU v7x, 256 devices: a whole 4x4x8 slice. The times are simulated.
256 devices in a mesh: dp: 32 (over y, x, core), shard: 8 (over z).
Axes of the slice: x: 4, y: 4, z: 8, core: 2. Of those that a mesh axis runs over, the one named last changes fastest.
Arguments:
- grads: bfloat16 [2, 32, 4096, 4096], P(None, 'dp', 'shard'), may hold values from -0.5 to 0.5
- basis: float32 [2, 4096, 256], P(None, 'shard'), may hold values from -0.375 to 0.375
- weight: float32 [2, 8, 32, 16, 4096], P(None, 'shard', 'dp'), may hold values from -6 to 6
- moment_m: float32 [2, 4096, 256], P(None, 'dp'), may hold values from -6 to 6
- moment_v: float32 [2, 4096, 256], P(None, 'dp'), may hold values from 0.25 to 4
Outputs:
- new_weight: float32 [2, 8, 32, 16, 4096], P(None, 'shard', 'dp')
- new_m: float32 [2, 4096, 256], P(None, 'dp')
- new_v: float32 [2, 4096, 256], P(None, 'dp')
- new_basis: float32 [2, 4096, 256], P(None, 'shard')
All inputs are finite; a program needn't handle non-finite values.
Results may differ from a plain program's by a relative error of at most 0.0036.
Values may be sent and summed in bfloat16 or wider, within the bound.
A program may use at most 64 MiB of HBM per device.

v0:
```python
import jax
import jax.numpy as jnp
from jax import lax
from jax.sharding import PartitionSpec as P

MATS = 2
NS_STEPS = 5


def adam_step(moment_m, moment_v, projected):
    next_m = 0.9 * moment_m + 0.1 * projected
    next_v = 0.999 * moment_v + 0.001 * projected * projected
    update = 2.0 * (next_m / (1.0 - 0.9**10)) / (jnp.sqrt(next_v / (1.0 - 0.999**10)) + 1e-08)
    return (next_m, next_v, update)


def ns_turn(iterate, gram):
    return 1.5 * iterate - 0.5 * jnp.dot(iterate, gram, precision=lax.Precision.HIGHEST)


def shards(grads, basis, weight, moment_m, moment_v):
    group_index = lax.axis_index("dp")
    rows_weight = weight.shape[3]
    weights_out, firsts, seconds, bases = ([], [], [], [])
    for matrix in range(MATS):
        gradient = grads[matrix, 0]
        basis_local = basis[matrix]
        basis_bf = basis_local.astype(jnp.bfloat16)
        partial_sum = lax.psum_scatter(
            lax.dot_general(
                gradient, basis_bf, (((0,), (0,)), ((), ())), preferred_element_type=jnp.float32
            ),
            "dp",
            scatter_dimension=0,
            tiled=True,
        )
        projected = lax.psum(partial_sum, "shard")
        next_m, next_v, update = adam_step(moment_m[matrix], moment_v[matrix], projected)
        full_update = lax.all_gather(update, "dp", axis=0, tiled=True)
        basis_rows = lax.dynamic_slice_in_dim(
            basis_local, group_index * rows_weight, rows_weight, 0
        )
        delta = jnp.dot(basis_rows, full_update.T, precision=lax.Precision.HIGHEST)
        weights_out.append((weight[matrix, 0, 0] - delta).reshape(weight.shape[1:]))
        projected_bf = projected.astype(jnp.bfloat16)
        refresh_part = jnp.dot(
            gradient,
            lax.all_gather(projected_bf, "dp", axis=0, tiled=True),
            preferred_element_type=jnp.float32,
        )
        refresh = lax.psum(refresh_part, "dp")
        total_sq = lax.psum(jnp.sum(refresh * refresh), "shard")
        iterate = refresh / jnp.sqrt(total_sq + 1e-06)
        first_turn = 0
        for step in range(first_turn, NS_STEPS):
            gram = lax.psum(
                jnp.dot(iterate.T, iterate, precision=lax.Precision.HIGHEST).astype(jnp.bfloat16),
                "shard",
            ).astype(jnp.float32)
            iterate = ns_turn(iterate, gram)
        bases.append(iterate)
        firsts.append(next_m)
        seconds.append(next_v)
    return (jnp.stack(weights_out), jnp.stack(firsts), jnp.stack(seconds), jnp.stack(bases))


def solution(mesh):
    placed = (
        P(None, "dp", "shard", None),
        P(None, "shard", None),
        P(None, "shard", "dp", None, None),
        P(None, "dp", None),
        P(None, "dp", None),
    )
    return jax.shard_map(
        shards,
        mesh=mesh,
        in_specs=placed,
        out_specs=(
            P(None, "shard", "dp", None, None),
            P(None, "dp", None),
            P(None, "dp", None),
            P(None, "shard", None),
        ),
        check_vma=False,
    )
```

profile of v0, /device:TPU:1, one launch (start us, length us, event | category | flops | bytes accessed | tf_op | source)
XLA Modules:
  0.0 1018.5 jit_solution(8599303258596466312)
XLA Ops:
  7.2 5.5 fusion.4
  12.8 1.1 copy-done
  14.0 5.5 fusion.8
  19.6 85.4 %reduce-scatter.5.cloned.1.call-done = f32[128,256]{1,0:T(8,128)} async-done(((f32[4096,256]{1,0:T(8,128)}), f32[128,256]{1,0:T(8,128)}) %reduce-scatter.5.cloned.1.call-update) | async-done | bytes 131088 | tf_op jit(solution)/shard_map/reduce_scatter | solution.py:29
  104.9 93.3 %reduce-scatter.3.cloned.1.call-done = f32[128,256]{1,0:T(8,128)} async-done(((f32[4096,256]{1,0:T(8,128)}), f32[128,256]{1,0:T(8,128)}) %reduce-scatter.3.cloned.1.call-update) | async-done | bytes 131088 | tf_op jit(solution)/shard_map/reduce_scatter | solution.py:29
  198.3 71.4 %all-reduce.18.cloned.1.call-done = (f32[128,256]{1,0:T(8,128)}, f32[128,256]{1,0:T(8,128)}) async-done(((f32[128,256]{1,0:T(8,128)}, f32[128,256]{1,0:T(8,128)}), (f32[128,256]{1,0:T(8,128)}, f32[128,256]{1,0:T(8,128)})) %all-reduce.18.cloned.1.call-update) | async-done | bytes 262160 | tf_op jit(solution)/shard_map/psum | solution.py:37
  269.8 2.0 add_divide_fusion.1
  271.8 0.5 all-gather.11.cloned.1.call-update
  272.4 52.9 %all-gather.9.cloned.1.call-done = bf16[4096,256]{1,0:T(8,128)(2,1)} async-done(((bf16[128,256]{1,0:T(8,128)(2,1)}), bf16[4096,256]{1,0:T(8,128)(2,1)}) %all-gather.9.cloned.1.call-update) | async-done | bytes 2097168 | tf_op jit(solution)/shard_map/all_gather | solution.py:48
  325.3 4.9 fusion.14
  330.2 46.1 %all-gather.11.cloned.1.call-done = bf16[4096,256]{1,0:T(8,128)(2,1)} async-done(((bf16[128,256]{1,0:T(8,128)(2,1)}), bf16[4096,256]{1,0:T(8,128)(2,1)}) %all-gather.11.cloned.1.call-update) | async-done | bytes 2097168 | tf_op jit(solution)/shard_map/all_gather | solution.py:48
  376.3 4.9 fusion.17
  381.3 114.6 %all-reduce.16.cloned.1.call-done = (f32[512,256]{0,1:T(8,128)}, f32[512,256]{0,1:T(8,128)}) async-done(((f32[512,256]{0,1:T(8,128)}, f32[512,256]{0,1:T(8,128)}), (f32[512,256]{0,1:T(8,128)}, f32[512,256]{0,1:T(8,128)})) %all-reduce.16.cloned.1.call-update) | async-done | bytes 1048592 | tf_op jit(solution)/shard_map/psum | solution.py:51
  495.8 2.0 multiply_reduce_fusion
  497.8 14.3 %all-reduce.1 = (f32[]{:T(128)}, f32[]{:T(128)}) all-reduce(f32[]{:T(128)} %get-tuple-element.36, f32[]{:T(128)} %get-tuple-element.37), channel_id=1, replica_groups=mesh['dp'=32,'shard'=8] {'shard'}, use_global_device_ids=true, to_apply=%region_14.0 | all-reduce | flops 2 | bytes 16 | tf_op jit(solution)/shard_map/psum | solution.py:52
  513.5 2.5 convolution_convert_fusion.4
  516.1 2.5 convolution_convert_fusion.9
  518.6 68.6 %all-reduce.28.cloned.1.call-done = (bf16[256,256]{1,0:T(8,128)(2,1)}, bf16[256,256]{1,0:T(8,128)(2,1)}) async-done(((bf16[256,256]{1,0:T(8,128)(2,1)}, bf16[256,256]{1,0:T(8,128)(2,1)}), (bf16[256,256]{1,0:T(8,128)(2,1)}, bf16[256,256]{1,0:T(8,128)(2,1)})) %all-reduce.28.cloned.1.call-update) | async-done | bytes 262160 | tf_op jit(solution)/shard_map/psum | solution.py:56
  587.2 1.4 fusion.31
  588.6 1.4 fusion.25
  590.0 1.3 convolution_convert_fusion.3
  591.3 1.3 convolution_convert_fusion.8
  592.8 71.3 %all-reduce.26.cloned.1.call-done = (bf16[256,256]{1,0:T(8,128)(2,1)}, bf16[256,256]{1,0:T(8,128)(2,1)}) async-done(((bf16[256,256]{1,0:T(8,128)(2,1)}, bf16[256,256]{1,0:T(8,128)(2,1)}), (bf16[256,256]{1,0:T(8,128)(2,1)}, bf16[256,256]{1,0:T(8,128)(2,1)})) %all-reduce.26.cloned.1.call-update) | async-done | bytes 262160 | tf_op jit(solution)/shard_map/psum | solution.py:56
  664.2 1.4 fusion.24
  665.6 1.4 fusion.30
  667.0 1.3 convolution_convert_fusion.7
  668.2 1.3 convolution_convert_fusion.2
  669.6 71.5 %all-reduce.24.cloned.1.call-done = (bf16[256,256]{1,0:T(8,128)(2,1)}, bf16[256,256]{1,0:T(8,128)(2,1)}) async-done(((bf16[256,256]{1,0:T(8,128)(2,1)}, bf16[256,256]{1,0:T(8,128)(2,1)}), (bf16[256,256]{1,0:T(8,128)(2,1)}, bf16[256,256]{1,0:T(8,128)(2,1)})) %all-reduce.24.cloned.1.call-update) | async-done | bytes 262160 | tf_op jit(solution)/shard_map/psum | solution.py:56
  741.1 1.4 fusion.23
  742.5 1.4 fusion.29
  743.9 1.3 convolution_convert_fusion.6
  745.1 1.3 convolution_convert_fusion.1
  746.5 71.5 %all-reduce.22.cloned.1.call-done = (bf16[256,256]{1,0:T(8,128)(2,1)}, bf16[256,256]{1,0:T(8,128)(2,1)}) async-done(((bf16[256,256]{1,0:T(8,128)(2,1)}, bf16[256,256]{1,0:T(8,128)(2,1)}), (bf16[256,256]{1,0:T(8,128)(2,1)}, bf16[256,256]{1,0:T(8,128)(2,1)})) %all-reduce.22.cloned.1.call-update) | async-done | bytes 262160 | tf_op jit(solution)/shard_map/psum | solution.py:56
  818.0 1.4 fusion.22
  819.4 1.4 fusion.28
  820.8 1.3 convolution_convert_fusion.5
  822.0 1.3 convolution_convert_fusion
  824.7 1.3 fusion.50
  826.0 0.8 pad_maximum_fusion.2
  826.8 68.2 %all-reduce.20.cloned.1.call-done = (bf16[256,256]{1,0:T(8,128)(2,1)}, bf16[256,256]{1,0:T(8,128)(2,1)}) async-done(((bf16[256,256]{1,0:T(8,128)(2,1)}, bf16[256,256]{1,0:T(8,128)(2,1)}), (bf16[256,256]{1,0:T(8,128)(2,1)}, bf16[256,256]{1,0:T(8,128)(2,1)})) %all-reduce.20.cloned.1.call-update) | async-done | bytes 262160 | tf_op jit(solution)/shard_map/psum | solution.py:56
  895.0 1.4 fusion.21
  896.4 1.4 fusion.27
  897.8 1.3 copy.19
  899.2 53.3 %all-gather.5.cloned.1.call-done = f32[4096,256]{1,0:T(8,128)} async-done(((f32[128,256]{1,0:T(8,128)}), f32[4096,256]{1,0:T(8,128)}) %all-gather.5.cloned.1.call-update) | async-done | bytes 4194320 | tf_op jit(solution)/shard_map/all_gather | solution.py:39
  952.4 5.7 fusion.1
  958.1 47.4 %all-gather.7.cloned.1.call-done = f32[4096,256]{1,0:T(8,128)} async-done(((f32[128,256]{1,0:T(8,128)}), f32[4096,256]{1,0:T(8,128)}) %all-gather.7.cloned.1.call-update) | async-done | bytes 4194320 | tf_op jit(solution)/shard_map/all_gather | solution.py:39
  1005.5 5.7 fusion
  1011.1 0.8 pad_maximum_fusion.1
  (37 shorter events, 2.2 us)
Async XLA Ops:
  7.2 97.8 %reduce-scatter.5.cloned.1.call-start = ((), (), s32[]{:S(2)}) async-start(), calls=%async_computation.4 | async-start | bytes 4325376 | tf_op jit(solution)/shard_map/reduce_scatter | solution.py:29
  12.8 1.2 copy-start
  12.8 185.5 %reduce-scatter.3.cloned.1.call-start = ((), (), s32[]{:S(2)}) async-start(), calls=%async_computation.2 | async-start | bytes 4325376 | tf_op jit(solution)/shard_map/reduce_scatter | solution.py:29
  19.5 250.3 %copy-start.4 = (f32[2,128,256]{2,1,0:T(8,128)S(1)}, f32[2,128,256]{2,1,0:T(8,128)}, u32[]{:S(2)}) copy-start(f32[2,128,256]{2,1,0:T(8,128)} %param.8) | copy-start | bytes 786436
  19.5 250.3 %copy-start.5 = (f32[2,128,256]{2,1,0:T(8,128)S(1)}, f32[2,128,256]{2,1,0:T(8,128)}, u32[]{:S(2)}) copy-start(f32[2,128,256]{2,1,0:T(8,128)} %param.9) | copy-start | bytes 786436
  19.5 250.2 %all-reduce.18.cloned.1.call-start = ((), (), s32[]{:S(2)}) async-start(), calls=%async_computation.9 | async-start | bytes 524288 | tf_op jit(solution)/shard_map/psum | solution.py:37
  198.3 127.0 %all-gather.9.cloned.1.call-start = ((), (), s32[]{:S(2)}) async-start(), calls=%async_computation.6 | async-start | bytes 2162688 | tf_op jit(solution)/shard_map/all_gather | solution.py:48
  271.7 104.5 %all-gather.11.cloned.1.call-start = ((), (), s32[]{:S(2)}) async-start(), calls=%async_computation.7 | async-start | bytes 2162688 | tf_op jit(solution)/shard_map/all_gather | solution.py:48
  272.3 223.5 %all-reduce.16.cloned.1.call-start = ((), (), s32[]{:S(2)}) async-start(), calls=%async_computation.8 | async-start | bytes 2097152 | tf_op jit(solution)/shard_map/psum | solution.py:51
  381.2 206.0 %all-reduce.28.cloned.1.call-start = ((), (), s32[]{:S(2)}) async-start(), calls=%async_computation.14 | async-start | bytes 524288 | tf_op jit(solution)/shard_map/psum | solution.py:56
  495.8 91.4 %copy-start.3 = (f32[512,256]{0,1:T(8,128)S(1)}, f32[512,256]{0,1:T(8,128)}, u32[]{:S(2)}) copy-start(f32[512,256]{0,1:T(8,128)} %get-tuple-element.9) | copy-start | bytes 1572868
  497.8 90.8 %copy-start.2 = (f32[512,256]{0,1:T(8,128)S(1)}, f32[512,256]{0,1:T(8,128)}, u32[]{:S(2)}) copy-start(f32[512,256]{0,1:T(8,128)} %get-tuple-element.8) | copy-start | bytes 1572868
  518.6 145.6 %all-reduce.26.cloned.1.call-start = ((), (), s32[]{:S(2)}) async-start(), calls=%async_computation.13 | async-start | bytes 524288 | tf_op jit(solution)/shard_map/psum | solution.py:56
  592.6 148.5 %all-reduce.24.cloned.1.call-start = ((), (), s32[]{:S(2)}) async-start(), calls=%async_computation.12 | async-start | bytes 524288 | tf_op jit(solution)/shard_map/psum | solution.py:56
  669.5 148.5 %all-reduce.22.cloned.1.call-start = ((), (), s32[]{:S(2)}) async-start(), calls=%async_computation.11 | async-start | bytes 524288 | tf_op jit(solution)/shard_map/psum | solution.py:56
  746.4 148.5 %all-reduce.20.cloned.1.call-start = ((), (), s32[]{:S(2)}) async-start(), calls=%async_computation.10 | async-start | bytes 524288 | tf_op jit(solution)/shard_map/psum | solution.py:56
  823.3 129.1 %all-gather.5.cloned.1.call-start = ((), (), s32[]{:S(2)}) async-start(), calls=%async_computation.3 | async-start | bytes 4325376 | tf_op jit(solution)/shard_map/all_gather | solution.py:39
  823.9 181.6 %all-gather.7.cloned.1.call-start = ((), (), s32[]{:S(2)}) async-start(), calls=%async_computation.5 | async-start | bytes 4325376 | tf_op jit(solution)/shard_map/all_gather | solution.py:39
  825.9 126.5 %copy-start.1 = (f32[2,1,1,16,4096]{4,3,2,1,0:T(8,128)S(1)}, f32[2,1,1,16,4096]{4,3,2,1,0:T(8,128)}, u32[]{:S(2)}) copy-start(f32[2,1,1,16,4096]{4,3,2,1,0:T(8,128)} %param.7) | copy-start | bytes 1572868
Sparse Core Ops, SparseCore 0:
  12.9 91.9 reduce-scatter.4
  108.9 89.3 reduce-scatter.2
  200.6 69.0 all-reduce.17
  272.7 52.5 all-gather.8
  328.3 47.9 all-gather.10
  381.3 114.4 all-reduce.15
  518.7 68.4 all-reduce.27
  592.7 71.3 all-reduce.25
  669.6 71.3 all-reduce.23
  746.5 71.3 all-reduce.21
  823.5 71.4 all-reduce.19
  897.4 54.9 all-gather.4
  955.0 50.4 all-gather.6
where the time goes:
time: 1020 us
  waiting for transfers between devices  917 us (90%)
  matrix products  61.3 us (6%)
  between operations  15.4 us (2%)
  blocking collectives  14.3 us (1%)
    psum x5, waiting for transfers between devices, shards(): lax.psum(jnp.dot(iterate.T, iterate, precision=lax.Precision.HIGHEST).ast...  351 us
    reduce_scatter x2, waiting for transfers between devices, shards(): lax.psum_scatter(lax.dot_general(gradient, basis_bf, (((0,), (0,)), ((),...  179 us
    psum x1, waiting for transfers between devices, shards(): refresh = lax.psum(refresh_part, 'dp')  115 us
    all_gather x2, waiting for transfers between devices, shards(): full_update = lax.all_gather(update, 'dp', axis=0, tiled=True)  101 us
    all_gather x2, waiting for transfers between devices, shards(): lax.all_gather(projected_bf, 'dp', axis=0, tiled=True)  99 us
    psum x1, waiting for transfers between devices, shards(): projected = lax.psum(partial_sum, 'shard')  71.4 us
  transfers between devices with their start and end apart: 13, of which 13 were waited for; matrix products, arithmetic and copies ran while one was open for 2% of the time, Pallas kernels for 0%

commit v1 on v0

--- a/solution.py
+++ b/solution.py
@@ -5,6 +5,17 @@
 
 MATS = 2
 NS_STEPS = 5
+
+
+def cubes_search(page):
+    a_name = "shard"
+    cores_n = jax.lax.axis_size(a_name)
+    found_now = page
+    for dd in [t for t in (1, 2, 4, 8, 16) if t < cores_n]:
+        found_now = found_now + jax.lax.ppermute(
+            found_now, a_name, [(d, d ^ dd) for d in range(cores_n)]
+        )
+    return found_now
 
 
 def adam_step(moment_m, moment_v, projected):
@@ -34,7 +45,7 @@
             scatter_dimension=0,
             tiled=True,
         )
-        projected = lax.psum(partial_sum, "shard")
+        projected = cubes_search(partial_sum)
         next_m, next_v, update = adam_step(moment_m[matrix], moment_v[matrix], projected)
         full_update = lax.all_gather(update, "dp", axis=0, tiled=True)
         basis_rows = lax.dynamic_slice_in_dim(

time: 1020 us -> 946 us (0.927)
  waiting for transfers between devices: 917 us -> 823 us
  starting transfers between devices: 0.93 us -> 19.3 us
    psum x1 -> x0, waiting for transfers between devices: 71.4 us -> none  [shards(): projected = lax.psum(partial_sum, 'shard')]
    reduce_scatter x2, waiting for transfers between devices: 179 us -> 159 us  [shards(): lax.psum_scatter(lax.dot_general(gradient, basis_bf, (((0,), (0,)), ((),...]
    all_gather x2, waiting for transfers between devices: 99 us -> 79.5 us  [shards(): lax.all_gather(projected_bf, 'dp', axis=0, tiled=True)]
    ppermute x0 -> x6, starting transfers between devices: none -> 18.4 us  [cubes_search(): jax.lax.ppermute(found_now, a_name, [(d, d ^ dd) for d in range(cores_n)])]
    ppermute x0 -> x6, waiting for transfers between devices: none -> 18.1 us  [cubes_search(): jax.lax.ppermute(found_now, a_name, [(d, d ^ dd) for d in range(cores_n)])]
  transfers between devices with their start and end apart: 13 -> 18, of which waited for: 13 -> 18; matrix products, arithmetic and copies ran while one was open for 2% -> 3% of each run, Pallas kernels for 0% -> 0%
where the time goes in v1:
time: 946 us; the launch traced here: 945 us
  waiting for transfers between devices  823 us (87%)
  matrix products  60.4 us (6%)
  starting transfers between devices  19.3 us (2%)
  between operations  15.8 us (2%)
  blocking collectives  14.3 us (2%)
  other arithmetic  10 us (1%)
    psum x5, waiting for transfers between devices, shards(): lax.psum(jnp.dot(iterate.T, iterate, precision=lax.Precision.HIGHEST).ast...  350 us
    reduce_scatter x2, waiting for transfers between devices, shards(): lax.psum_scatter(lax.dot_general(gradient, basis_bf, (((0,), (0,)), ((),...  159 us
    psum x1, waiting for transfers between devices, shards(): refresh = lax.psum(refresh_part, 'dp')  115 us
    all_gather x2, waiting for transfers between devices, shards(): full_update = lax.all_gather(update, 'dp', axis=0, tiled=True)  101 us
    all_gather x2, waiting for transfers between devices, shards(): lax.all_gather(projected_bf, 'dp', axis=0, tiled=True)  79.5 us
  transfers between devices with their start and end apart: 18, of which 18 were waited for; matrix products, arithmetic and copies ran while one was open for 3% of the time, Pallas kernels for 0%

profile of v1, /device:TPU:1, one launch (start us, length us, event | category | flops | bytes accessed | tf_op | source)
XLA Modules:
  0.0 945.1 jit_solution(8075530683474858713)
XLA Ops:
  7.2 5.6 fusion.4
  14.1 5.4 fusion.8
  19.6 85.4 %reduce-scatter.5.cloned.1.call-done = f32[128,256]{1,0:T(8,128)} async-done(((f32[4096,256]{1,0:T(8,128)}), f32[128,256]{1,0:T(8,128)}) %reduce-scatter.5.cloned.1.call-update) | async-done | bytes 131088 | tf_op jit(solution)/shard_map/reduce_scatter | solution.py:40
  105.0 1.3 collective-permute-start.3
  106.3 2.7 collective-permute-done.3
  110.0 2.4 collective-permute-start.4
  112.3 3.9 collective-permute-done.4
  116.2 5.5 collective-permute-start.5
  121.7 2.5 collective-permute-done.5
  124.9 73.4 %reduce-scatter.3.cloned.1.call-done = f32[128,256]{1,0:T(8,128)} async-done(((f32[4096,256]{1,0:T(8,128)}), f32[128,256]{1,0:T(8,128)}) %reduce-scatter.3.cloned.1.call-update) | async-done | bytes 131088 | tf_op jit(solution)/shard_map/reduce_scatter | solution.py:40
  198.3 1.3 collective-permute-start
  199.6 2.7 collective-permute-done
  203.3 2.4 collective-permute-start.1
  205.7 3.9 collective-permute-done.1
  209.5 5.5 collective-permute-start.2
  215.1 2.5 collective-permute-done.2
  218.3 33.4 %all-gather.11.cloned.1.call-done = bf16[4096,256]{1,0:T(8,128)(2,1)} async-done(((bf16[128,256]{1,0:T(8,128)(2,1)}), bf16[4096,256]{1,0:T(8,128)(2,1)}) %all-gather.11.cloned.1.call-update) | async-done | bytes 2097168 | tf_op jit(solution)/shard_map/all_gather | solution.py:59
  251.6 4.9 fusion.17
  256.6 46.1 %all-gather.9.cloned.1.call-done = bf16[4096,256]{1,0:T(8,128)(2,1)} async-done(((bf16[128,256]{1,0:T(8,128)(2,1)}), bf16[4096,256]{1,0:T(8,128)(2,1)}) %all-gather.9.cloned.1.call-update) | async-done | bytes 2097168 | tf_op jit(solution)/shard_map/all_gather | solution.py:59
  302.6 4.9 fusion.14
  307.6 114.6 %all-reduce.14.cloned.1.call-done = (f32[512,256]{0,1:T(8,128)}, f32[512,256]{0,1:T(8,128)}) async-done(((f32[512,256]{0,1:T(8,128)}, f32[512,256]{0,1:T(8,128)}), (f32[512,256]{0,1:T(8,128)}, f32[512,256]{0,1:T(8,128)})) %all-reduce.14.cloned.1.call-update) | async-done | bytes 1048592 | tf_op jit(solution)/shard_map/psum | solution.py:62
  422.2 2.0 multiply_reduce_fusion
  424.2 14.3 %all-reduce.1 = (f32[]{:T(128)}, f32[]{:T(128)}) all-reduce(f32[]{:T(128)} %get-tuple-element.36, f32[]{:T(128)} %get-tuple-element.37), channel_id=1, replica_groups=mesh['dp'=32,'shard'=8] {'shard'}, use_global_device_ids=true, to_apply=%region_12.0 | all-reduce | flops 2 | bytes 16 | tf_op jit(solution)/shard_map/psum | solution.py:63
  439.2 2.5 convolution_convert_fusion.4
  442.5 2.5 convolution_convert_fusion.9
  445.2 68.4 %all-reduce.24.cloned.1.call-done = (bf16[256,256]{1,0:T(8,128)(2,1)}, bf16[256,256]{1,0:T(8,128)(2,1)}) async-done(((bf16[256,256]{1,0:T(8,128)(2,1)}, bf16[256,256]{1,0:T(8,128)(2,1)}), (bf16[256,256]{1,0:T(8,128)(2,1)}, bf16[256,256]{1,0:T(8,128)(2,1)})) %all-reduce.24.cloned.1.call-update) | async-done | bytes 262160 | tf_op jit(solution)/shard_map/psum | solution.py:67
  513.6 1.4 fusion.25
  515.0 1.3 convolution_convert_fusion.3
  518.2 71.5 %all-reduce.22.cloned.1.call-done = (bf16[256,256]{1,0:T(8,128)(2,1)}, bf16[256,256]{1,0:T(8,128)(2,1)}) async-done(((bf16[256,256]{1,0:T(8,128)(2,1)}, bf16[256,256]{1,0:T(8,128)(2,1)}), (bf16[256,256]{1,0:T(8,128)(2,1)}, bf16[256,256]{1,0:T(8,128)(2,1)})) %all-reduce.22.cloned.1.call-update) | async-done | bytes 262160 | tf_op jit(solution)/shard_map/psum | solution.py:67
  589.7 1.4 fusion.24
  591.1 1.3 convolution_convert_fusion.2
  592.4 1.4 fusion.30
  595.1 71.6 %all-reduce.20.cloned.1.call-done = (bf16[256,256]{1,0:T(8,128)(2,1)}, bf16[256,256]{1,0:T(8,128)(2,1)}) async-done(((bf16[256,256]{1,0:T(8,128)(2,1)}, bf16[256,256]{1,0:T(8,128)(2,1)}), (bf16[256,256]{1,0:T(8,128)(2,1)}, bf16[256,256]{1,0:T(8,128)(2,1)})) %all-reduce.20.cloned.1.call-update) | async-done | bytes 262160 | tf_op jit(solution)/shard_map/psum | solution.py:67
  666.7 1.4 fusion.23
  669.3 1.4 fusion.29
  672.1 71.6 %all-reduce.18.cloned.1.call-done = (bf16[256,256]{1,0:T(8,128)(2,1)}, bf16[256,256]{1,0:T(8,128)(2,1)}) async-done(((bf16[256,256]{1,0:T(8,128)(2,1)}, bf16[256,256]{1,0:T(8,128)(2,1)}), (bf16[256,256]{1,0:T(8,128)(2,1)}, bf16[256,256]{1,0:T(8,128)(2,1)})) %all-reduce.18.cloned.1.call-update) | async-done | bytes 262160 | tf_op jit(solution)/shard_map/psum | solution.py:67
  743.7 1.4 fusion.22
  746.3 1.4 fusion.28
  749.1 2.0 add_divide_fusion.1
  751.8 1.9 pad_maximum_fusion.2
  753.7 67.0 %all-reduce.16.cloned.1.call-done = (bf16[256,256]{1,0:T(8,128)(2,1)}, bf16[256,256]{1,0:T(8,128)(2,1)}) async-done(((bf16[256,256]{1,0:T(8,128)(2,1)}, bf16[256,256]{1,0:T(8,128)(2,1)}), (bf16[256,256]{1,0:T(8,128)(2,1)}, bf16[256,256]{1,0:T(8,128)(2,1)})) %all-reduce.16.cloned.1.call-update) | async-done | bytes 262160 | tf_op jit(solution)/shard_map/psum | solution.py:67
  820.6 1.4 fusion.21
  822.0 1.4 fusion.27
  823.5 1.3 copy.19
  824.8 53.4 %all-gather.7.cloned.1.call-done = f32[4096,256]{1,0:T(8,128)} async-done(((f32[128,256]{1,0:T(8,128)}), f32[4096,256]{1,0:T(8,128)}) %all-gather.7.cloned.1.call-update) | async-done | bytes 4194320 | tf_op jit(solution)/shard_map/all_gather | solution.py:50
  878.2 5.7 fusion
  883.9 47.8 %all-gather.5.cloned.1.call-done = f32[4096,256]{1,0:T(8,128)} async-done(((f32[128,256]{1,0:T(8,128)}), f32[4096,256]{1,0:T(8,128)}) %all-gather.5.cloned.1.call-update) | async-done | bytes 4194320 | tf_op jit(solution)/shard_map/all_gather | solution.py:50
  931.7 5.7 fusion.1
  (50 shorter events, 14.8 us)
Async XLA Ops:
  7.2 97.8 %reduce-scatter.5.cloned.1.call-start = ((), (), s32[]{:S(2)}) async-start(), calls=%async_computation.4 | async-start | bytes 4325376 | tf_op jit(solution)/shard_map/reduce_scatter | solution.py:40
  12.8 1.2 copy-start
  12.9 185.5 %reduce-scatter.3.cloned.1.call-start = ((), (), s32[]{:S(2)}) async-start(), calls=%async_computation.2 | async-start | bytes 4325376 | tf_op jit(solution)/shard_map/reduce_scatter | solution.py:40
  19.5 232.1 %all-gather.11.cloned.1.call-start = ((), (), s32[]{:S(2)}) async-start(), calls=%async_computation.7 | async-start | bytes 2162688 | tf_op jit(solution)/shard_map/all_gather | solution.py:59
  105.0 4.0 collective-permute-start.3
  110.0 6.2 collective-permute-start.4
  116.2 8.0 collective-permute-start.5
  124.9 177.8 %all-gather.9.cloned.1.call-start = ((), (), s32[]{:S(2)}) async-start(), calls=%async_computation.6 | async-start | bytes 2162688 | tf_op jit(solution)/shard_map/all_gather | solution.py:59
  198.3 4.0 collective-permute-start
  203.3 6.2 collective-permute-start.1
  209.5 8.0 collective-permute-start.2
  218.2 204.0 %all-reduce.14.cloned.1.call-start = ((), (), s32[]{:S(2)}) async-start(), calls=%async_computation.8 | async-start | bytes 2097152 | tf_op jit(solution)/shard_map/psum | solution.py:62
  307.6 206.0 %all-reduce.24.cloned.1.call-start = ((), (), s32[]{:S(2)}) async-start(), calls=%async_computation.13 | async-start | bytes 524288 | tf_op jit(solution)/shard_map/psum | solution.py:67
  422.2 91.4 %copy-start.3 = (f32[512,256]{0,1:T(8,128)S(1)}, f32[512,256]{0,1:T(8,128)}, u32[]{:S(2)}) copy-start(f32[512,256]{0,1:T(8,128)} %get-tuple-element.8) | copy-start | bytes 1572868
  441.7 74.6 %copy-start.2 = (f32[512,256]{0,1:T(8,128)S(1)}, f32[512,256]{0,1:T(8,128)}, u32[]{:S(2)}) copy-start(f32[512,256]{0,1:T(8,128)} %get-tuple-element.9) | copy-start | bytes 1572868
  445.0 144.7 %all-reduce.22.cloned.1.call-start = ((), (), s32[]{:S(2)}) async-start(), calls=%async_computation.12 | async-start | bytes 524288 | tf_op jit(solution)/shard_map/psum | solution.py:67
  513.6 2.7 copy-start.4
  518.1 148.5 %all-reduce.20.cloned.1.call-start = ((), (), s32[]{:S(2)}) async-start(), calls=%async_computation.11 | async-start | bytes 524288 | tf_op jit(solution)/shard_map/psum | solution.py:67
  595.1 148.6 %all-reduce.18.cloned.1.call-start = ((), (), s32[]{:S(2)}) async-start(), calls=%async_computation.10 | async-start | bytes 524288 | tf_op jit(solution)/shard_map/psum | solution.py:67
  672.0 148.6 %all-reduce.16.cloned.1.call-start = ((), (), s32[]{:S(2)}) async-start(), calls=%async_computation.9 | async-start | bytes 524288 | tf_op jit(solution)/shard_map/psum | solution.py:67
  749.0 129.2 %all-gather.7.cloned.1.call-start = ((), (), s32[]{:S(2)}) async-start(), calls=%async_computation.5 | async-start | bytes 4325376 | tf_op jit(solution)/shard_map/all_gather | solution.py:50
  751.1 180.6 %all-gather.5.cloned.1.call-start = ((), (), s32[]{:S(2)}) async-start(), calls=%async_computation.3 | async-start | bytes 4325376 | tf_op jit(solution)/shard_map/all_gather | solution.py:50
  751.8 126.5 %copy-start.1 = (f32[2,1,1,16,4096]{4,3,2,1,0:T(8,128)S(1)}, f32[2,1,1,16,4096]{4,3,2,1,0:T(8,128)}, u32[]{:S(2)}) copy-start(f32[2,1,1,16,4096]{4,3,2,1,0:T(8,128)} %param.7) | copy-start | bytes 1572868
Sparse Core Ops, SparseCore 0:
  13.0 91.9 reduce-scatter.4
  108.9 89.3 reduce-scatter.2
  201.5 50.1 all-gather.10
  254.6 47.9 all-gather.8
  307.7 114.4 all-reduce.13
  445.1 68.4 all-reduce.23
  518.3 71.3 all-reduce.21
  595.2 71.4 all-reduce.19
  672.2 71.4 all-reduce.17
  749.1 71.4 all-reduce.15
  823.2 54.9 all-gather.6
  881.2 50.4 all-gather.4
